TPU v7x, 128 devices: a whole 4x4x4 slice. The times are simulated.
128 devices in a mesh: row: 16 (over x, y), col: 8 (over z, core).
Axes of the slice: x: 4, y: 4, z: 4, core: 2. Of those that a mesh axis runs over, the one named last changes fastest.
Arguments:
- orbitals: bfloat16 [131072, 512], P(('row', 'col')), may hold values from -6 to 6
- coulomb: bfloat16 [32768, 32768], P('row', 'col'), may hold values from -0.0014648438 to 0.0014648438
- interp: bfloat16 [131072, 1024], P(('row', 'col')), may hold values from -0.1875 to 0.1875
- box_counts: int32 [128], replicated, may hold values from 1 to 768, 32768 in all
- owner_map: int32 [32768], replicated, may hold values from 0 to 32767, as said below
- grid_rows: int32 [128, 1024], P(('row', 'col')), may hold values from 0 to 1023, each once within a row
- listed: int32 [128, 1024], P(('row', 'col')), may hold values from 0 to 255
Outputs:
- exchange_action: float32 [131072, 512], P(('row', 'col'))
Inputs may be any that keep to these rules, and one draw needn't show every extreme that they name: `box_counts`: the counts sum to 32768; the largest is exactly 768. `owner_map`: A permutation of the 32768 positions; a point's owner is position // 256. No box holds more than 6 points of one owner, and the box with 768 points holds exactly 6 of some owner. `grid_rows`: each row is a permutation.
All inputs are finite; a program needn't handle non-finite values.
Results may differ from a plain program's by a relative error of at most 0.012.
Values may be sent and summed in bfloat16 or wider, within the bound.
A program may use at most 128 MiB of HBM per device.

v0:
```python
import jax
import jax.numpy as jnp
from jax import lax
from jax.sharding import PartitionSpec as P

NORB = 512
LIST = 1024
OWN = 256
SLOTS = 768


def copy_for_each(x, axis):
    copies = jnp.broadcast_to(x, (lax.axis_size(axis), *x.shape))
    return lax.all_to_all(copies, axis, split_axis=0, concat_axis=0, tiled=True)


def in_order(parts, dim):
    parts = jnp.moveaxis(parts, 0, dim)
    dims = parts.shape
    return parts.reshape(*dims[:dim], dims[dim] * dims[dim + 1], *dims[dim + 2 :])


def gather_directly(x, axis, dim):
    parts = copy_for_each(x, axis)
    return in_order(parts, dim)


def add_block(shard_rows, left_rows, kernel_tile):
    pair_tile = jnp.einsum(
        "ak,bk->ab", left_rows, shard_rows, preferred_element_type=jnp.float32
    ).astype(jnp.bfloat16)
    weighted = (pair_tile.astype(jnp.float32) * kernel_tile.astype(jnp.float32)).astype(
        jnp.bfloat16
    )
    return jnp.dot(weighted, shard_rows, preferred_element_type=jnp.float32)


def shards(orbitals, coulomb, interp, box_counts, owner_map, grid_rows, listed):
    row_count = lax.axis_size("row")
    col_count = lax.axis_size("col")
    box_total = row_count * col_count
    point_total = OWN * box_total
    capacity = (SLOTS + box_total - 1) // box_total
    per_owner = LIST // box_total
    my_box = lax.axis_index("row") * col_count + lax.axis_index("col")
    box_ids = jnp.arange(box_total, dtype=jnp.int32)
    first_point = jnp.sum(jnp.where(box_ids < my_box, box_counts, 0))
    my_count = jnp.sum(jnp.where(box_ids == my_box, box_counts, 0))
    slot_ids = jnp.arange(SLOTS, dtype=jnp.int32)
    is_live = slot_ids < my_count
    listing = jnp.minimum(first_point + slot_ids, point_total - 1)
    owner_ids = owner_map[listing] // OWN
    matches = (
        (owner_ids[:, None] == owner_ids[None, :])
        & is_live[None, :]
        & (slot_ids[None, :] < slot_ids[:, None])
    )
    pair_rank = jnp.sum(matches.astype(jnp.int32), axis=1)
    target = jnp.where(is_live, owner_ids * capacity + pair_rank, box_total * capacity)
    dest_slots = jnp.arange(box_total * capacity, dtype=jnp.int32)
    hits = target[None, :] == dest_slots[:, None]
    source_slot = jnp.sum(jnp.where(hits, slot_ids[None, :], 0), axis=1)
    filled = jnp.any(hits, axis=1)
    picked = orbitals[grid_rows[0, source_slot]]
    outgoing = jnp.where(filled[:, None], picked, jnp.zeros_like(picked))
    received = lax.all_to_all(
        outgoing.reshape(box_total, capacity, NORB),
        ("row", "col"),
        split_axis=0,
        concat_axis=0,
        tiled=True,
    )
    received = received.reshape(box_total * capacity, NORB)
    wanted_pos = my_box * OWN + jnp.arange(OWN, dtype=jnp.int32)
    all_listing = jnp.arange(point_total, dtype=jnp.int32)
    my_points = jnp.sum(
        jnp.where(owner_map[None, :] == wanted_pos[:, None], all_listing[None, :], 0), axis=1
    )
    box_ends = jnp.cumsum(box_counts)
    source = jnp.sum((my_points[:, None] >= box_ends[None, :]).astype(jnp.int32), axis=1)
    earlier = (source[:, None] == source[None, :]) & (my_points[None, :] < my_points[:, None])
    source_rank = jnp.sum(earlier.astype(jnp.int32), axis=1)
    owned_rows = received[source * capacity + source_rank]
    left_rows = gather_directly(owned_rows, "col", 0)
    partial_sums = add_block(
        lax.all_gather(owned_rows, "row", axis=0, tiled=True), left_rows, coulomb
    )
    owned_result = lax.psum_scatter(partial_sums, "col", scatter_dimension=0, tiled=True).astype(
        jnp.bfloat16
    )
    wanted = listed[0].reshape(box_total, per_owner)
    fetched = lax.all_to_all(
        owned_result[
            lax.all_to_all(wanted, ("row", "col"), split_axis=0, concat_axis=0, tiled=True)
        ],
        ("row", "col"),
        split_axis=0,
        concat_axis=0,
        tiled=True,
    )
    chosen_rows = fetched.reshape(LIST, NORB)
    return -jnp.dot(interp, chosen_rows, preferred_element_type=jnp.float32)


def solution(mesh):
    return jax.shard_map(
        shards,
        mesh=mesh,
        in_specs=(
            P(("row", "col"), None),
            P("row", "col"),
            P(("row", "col"), None),
            P(),
            P(),
            P(("row", "col"), None),
            P(("row", "col"), None),
        ),
        out_specs=P(("row", "col"), None),
        check_vma=False,
    )
```

profile of v0, /device:TPU:1, one launch (start us, length us, event | category | flops | bytes accessed | tf_op | source)
XLA Modules:
  0.0 216.9 jit_solution(2038270782259860773)
XLA Ops:
  6.5 1.5 fusion.12
  8.1 0.7 fusion.7
  8.8 4.7 %gather_fusion = s32[768]{0:T(1024)S(1)} fusion(s32[32768]{0:T(1024)} %param.11, s32[1024]{0:T(1024)S(1)} %pad_clamp_fusion.2), kind=kCustom, calls=%fused_computation | custom fusion | bytes 9216 | tf_op jit(solution)/shard_map/gather | solution.py:52
  13.5 0.7 iota_compare_fusion.2
  14.2 0.4 convert_reduce_fusion
  14.7 0.7 add_select_fusion.1
  15.3 0.3 select_reduce_fusion.1
  15.6 0.3 fusion.2
  16.0 4.7 %gather_fusion.1 = s32[768]{0:T(1024)S(1)} fusion(s32[1,1024]{1,0:T(1,128)S(1)} %copy-done.1, s32[768]{0:T(1024)S(1)} %fusion.11), kind=kCustom, calls=%fused_computation.1 | custom fusion | bytes 12288 | tf_op jit(solution)/shard_map/gather | solution.py:64
  20.7 3.3 %gather_fusion.2 = bf16[768,512]{1,0:T(8,128)(2,1)} fusion(bf16[1024,512]{1,0:T(8,128)(2,1)S(1)} %copy-done.3, s32[1024]{0:T(1024)S(1)} %pad_clamp_fusion.1), kind=kCustom, calls=%fused_computation.2 | custom fusion | bytes 1575936 | tf_op jit(solution)/shard_map/gather | solution.py:64
  24.1 1.3 gather.23
  25.6 1.2 broadcast_select_fusion
  26.8 12.0 %all-to-all-start = ((bf16[128,6,512]{2,1,0:T(8,128)(2,1)}), bf16[128,6,512]{2,1,0:T(8,128)(2,1)}, u32[]{:S(2)}, u32[]{:S(2)}) async-start(bf16[128,6,512]{2,1,0:T(8,128)(2,1)} %broadcast_select_fusion), calls=%async_computation | async-start | bytes 2097152 | tf_op jit(solution)/shard_map/all_to_all | solution.py:66
  38.8 4.6 %select_reduce_fusion = s32[256]{0:T(256)S(1)} fusion(s32[32768]{0:T(1024)S(1)} %copy-done.2, s32[256]{0:T(256)S(1)} %iota_add_fusion), kind=kLoop, calls=%fused_computation.6 | loop fusion | flops 25165568 | bytes 133120 | tf_op jit(solution)/shard_map/reduce_sum | solution.py:76
  43.8 0.2 convert_reduce_fusion.2
  44.0 0.2 convert_reduce_fusion.1
  44.3 13.4 %all-to-all-done = bf16[128,6,512]{2,1,0:T(8,128)(2,1)} async-done(((bf16[128,6,512]{2,1,0:T(8,128)(2,1)}), bf16[128,6,512]{2,1,0:T(8,128)(2,1)}, u32[]{:S(2)}, u32[]{:S(2)}) %all-to-all-start) | async-done | bytes 786464 | tf_op jit(solution)/shard_map/all_to_all | solution.py:66
  57.7 1.4 reshape.199
  59.0 1.9 gather_fusion.3
  61.0 1.1 broadcast_in_dim.79
  62.1 30.8 %all_to_all.27 = bf16[8,256,512]{2,1,0:T(8,128)(2,1)} all-to-all(bf16[8,256,512]{2,1,0:T(8,128)(2,1)S(1)} %broadcast_in_dim.79), channel_id=1, replica_groups=mesh['row'=16,'col'=8] {'col'}, dimensions={0} | all-to-all | bytes 4194304 | tf_op jit(solution)/shard_map/all_to_all | solution.py:14
  92.9 15.8 %all-gather.3.cloned.1.call-done = bf16[4096,512]{1,0:T(8,128)(2,1)} async-done(((bf16[256,512]{1,0:T(8,128)(2,1)}), bf16[4096,512]{1,0:T(8,128)(2,1)}) %all-gather.3.cloned.1.call-update) | async-done | bytes 4194320 | tf_op jit(solution)/shard_map/all_gather | solution.py:86
  108.7 26.1 %fusion = f32[2048,512]{1,0:T(8,128)} fusion(bf16[4096,512]{1,0:T(8,128)(2,1)} %all-gather.3.cloned.1.call-done, bf16[2048,4096]{1,0:T(8,128)(2,1)} %param.8, bf16[2048,512]{1,0:T(8,128)(2,1)} %bitcast.27), kind=kOutput, calls=%fused_computation.7 | convolution fusion | flops 17213423616 | bytes 27262976 | tf_op jit(solution)/shard_map/dot_general | solution.py:35
  134.8 0.5 broadcast.260
  135.5 0.7 reduce.10
  136.2 17.2 %all_to_all.28 = s32[128,1,8]{2,1,0:T(1,128)S(1)} all-to-all(s32[128,1,8]{2,1,0:T(1,128)S(1)} %bitcast.28), channel_id=1, replica_groups=mesh['row'=16,'col'=8] {'row','col'}, dimensions={0} | all-to-all | bytes 8192 | tf_op jit(solution)/shard_map/all_to_all | solution.py:94
  153.5 16.8 %reduce-scatter.2.cloned.1.call-done = f32[256,512]{1,0:T(8,128)} async-done(((f32[2048,512]{1,0:T(8,128)}), f32[256,512]{1,0:T(8,128)}) %reduce-scatter.2.cloned.1.call-update) | async-done | bytes 524304 | tf_op jit(solution)/shard_map/reduce_scatter | solution.py:88
  170.3 1.1 convert_element_type.31
  171.4 4.0 %gather_fusion.4 = bf16[1024,512]{1,0:T(8,128)(2,1)S(1)} fusion(bf16[256,512]{1,0:T(8,128)(2,1)S(1)} %convert_element_type.31, s32[1024]{0:T(1024)S(1)} %broadcast_clamp_fusion), kind=kCustom, calls=%fused_computation.4 | custom fusion | bytes 2101248 | tf_op jit(solution)/shard_map/gather | solution.py:93
  175.4 29.2 %all_to_all.29 = bf16[128,8,512]{2,1,0:T(8,128)(2,1)S(1)} all-to-all(bf16[128,8,512]{2,1,0:T(8,128)(2,1)S(1)} %bitcast.26), channel_id=1, replica_groups=mesh['row'=16,'col'=8] {'row','col'}, dimensions={0} | all-to-all | bytes 2097152 | tf_op jit(solution)/shard_map/all_to_all | solution.py:92
  204.5 2.6 %negate_bitcast_fusion = f32[1024,512]{0,1:T(8,128)} fusion(bf16[1024,1024]{1,0:T(8,128)(2,1)S(1)} %copy-done, bf16[128,8,512]{2,1,0:T(8,128)(2,1)S(1)} %all_to_all.29), kind=kOutput, calls=%fused_computation.15 | convolution fusion | flops 1074266112 | bytes 5242880 | tf_op jit(solution)/shard_map/dot_general | solution.py:102
  207.2 2.9 %copy.17 = f32[1024,512]{1,0:T(8,128)} copy(f32[1024,512]{0,1:T(8,128)} %negate_bitcast_fusion) | data formatting | bytes 4194304 | tf_op jit(solution)/shard_map/neg | solution.py:102
  (33 shorter events, 1.1 us)
Async XLA Ops:
  6.5 198.0 %copy-start = (bf16[1024,1024]{1,0:T(8,128)(2,1)S(1)}, bf16[1024,1024]{1,0:T(8,128)(2,1)}, u32[]{:S(2)}) copy-start(bf16[1024,1024]{1,0:T(8,128)(2,1)} %param.9) | copy-start | bytes 6291460
  6.5 9.5 %copy-start.1 = (s32[1,1024]{1,0:T(1,128)S(1)}, s32[1,1024]{1,0:T(1,128)}, u32[]{:S(2)}) copy-start(s32[1,1024]{1,0:T(1,128)} %param.12) | copy-start | bytes 12292
  13.5 7.3 %copy-start.3 = (bf16[1024,512]{1,0:T(8,128)(2,1)S(1)}, bf16[1024,512]{1,0:T(8,128)(2,1)}, u32[]{:S(2)}) copy-start(bf16[1024,512]{1,0:T(8,128)(2,1)} %param.7) | copy-start | bytes 3145732
  25.4 13.4 %copy-start.2 = (s32[32768]{0:T(1024)S(1)}, s32[32768]{0:T(1024)}, u32[]{:S(2)}) copy-start(s32[32768]{0:T(1024)} %param.11) | copy-start | bytes 393220
  25.4 18.0 %copy-start.5 = (s32[128]{0:T(128)S(1)}, s32[128]{0:T(128)}, u32[]{:S(2)}) copy-start(s32[128]{0:T(128)} %param.10) | copy-start | bytes 1540
  26.8 30.9 %all-to-all-start = ((bf16[128,6,512]{2,1,0:T(8,128)(2,1)}), bf16[128,6,512]{2,1,0:T(8,128)(2,1)}, u32[]{:S(2)}, u32[]{:S(2)}) async-start(bf16[128,6,512]{2,1,0:T(8,128)(2,1)} %broadcast_select_fusion), calls=%async_computation | async-start | bytes 2097152 | tf_op jit(solution)/shard_map/all_to_all | solution.py:66
  38.7 70.0 %all-gather.3.cloned.1.call-start = ((), (), s32[]{:S(2)}) async-start(), calls=%async_computation.6 | async-start | bytes 4456448 | tf_op jit(solution)/shard_map/all_gather | solution.py:86
  60.9 109.4 %reduce-scatter.2.cloned.1.call-start = ((), (), s32[]{:S(2)}) async-start(), calls=%async_computation.5 | async-start | bytes 4718592 | tf_op jit(solution)/shard_map/reduce_scatter | solution.py:88
  134.8 0.7 copy-start.4
Sparse Core Ops, SparseCore 0:
  61.0 47.5 all-gather.2
  134.9 35.3 reduce-scatter.1
where the time goes:
time: 217 us
  blocking collectives  77.1 us (36%)
  waiting for transfers between devices  46 us (21%)
  matrix products  28.8 us (13%)
  local copies, waits for them, and re-layouts  26.3 us (12%)
  between operations  13.7 us (6%)
  other arithmetic  13 us (6%)
  starting transfers between devices  12 us (6%)
    all_to_all x1, blocking collectives, copy_for_each(): return lax.all_to_all(copies, axis, split_axis=0, concat_axis=0, tiled=True)  30.8 us
    all_to_all x1, blocking collectives, shards(): lax.all_to_all(owned_result[lax.all_to_all(wanted, ('row', 'col'), split_...  29.2 us
    dot_general x1, matrix products, add_block(): return jnp.dot(weighted, shard_rows, preferred_element_type=jnp.float32)  26.1 us
    all_to_all x1, blocking collectives, shards(): lax.all_to_all(wanted, ('row', 'col'), split_axis=0, concat_axis=0, tiled...  17.2 us
    reduce_scatter x1, waiting for transfers between devices, shards(): lax.psum_scatter(partial_sums, 'col', scatter_dimension=0, tiled=True)  16.8 us
    all_gather x1, waiting for transfers between devices, shards(): lax.all_gather(owned_rows, 'row', axis=0, tiled=True)  15.8 us
    all_to_all x1, waiting for transfers between devices, shards(): lax.all_to_all(outgoing.reshape(box_total, capacity, NORB), ('row', 'col'...  13.4 us
    all_to_all x1, starting transfers between devices, shards(): lax.all_to_all(outgoing.reshape(box_total, capacity, NORB), ('row', 'col'...  12 us
  transfers between devices with their start and end apart: 3, of which 3 were waited for; matrix products, arithmetic and copies ran while one was open for 4% of the time, Pallas kernels for 0%

commit v1 on v0

--- a/solution.py
+++ b/solution.py
@@ -2,6 +2,7 @@
 import jax.numpy as jnp
 from jax import lax
 from jax.sharding import PartitionSpec as P
+from jax.lax import axis_index, axis_size, ppermute
 
 NORB = 512
 LIST = 1024
@@ -82,9 +83,24 @@
     source_rank = jnp.sum(earlier.astype(jnp.int32), axis=1)
     owned_rows = received[source * capacity + source_rank]
     left_rows = gather_directly(owned_rows, "col", 0)
-    partial_sums = add_block(
-        lax.all_gather(owned_rows, "row", axis=0, tiled=True), left_rows, coulomb
-    )
+
+    def set_the_patch(state, d0):
+        mesh_name = "row"
+        extent = axis_size(mesh_name)
+        f_next = range(extent)
+        oldest = map(lambda idx: (idx, (idx + 1) % extent), f_next)
+        rows = list(oldest)
+        ledger = list(map(lambda idx: (idx, (idx - 1) % extent), range(extent)))
+        v_now, odd = ([state], [state])
+        for _ in range(extent // 2):
+            v_now.append(ppermute(v_now[-1], mesh_name, rows))
+        for _ in [*range((extent - 1) // 2)]:
+            odd.append(ppermute(odd[-1], axis_name=mesh_name, perm=ledger))
+        mixed_arr = jnp.concatenate([*v_now[::-1], *odd[1:]], axis=d0)
+        small = axis_index(mesh_name)
+        return jnp.roll(mixed_arr, shift=(small - extent // 2) * state.shape[d0], axis=d0)
+
+    partial_sums = add_block(set_the_patch(owned_rows, 0), left_rows, coulomb)
     owned_result = lax.psum_scatter(partial_sums, "col", scatter_dimension=0, tiled=True).astype(
         jnp.bfloat16
     )

time: 217 us -> 287 us (1.32)
  starting transfers between devices: 12 us -> 61.5 us
  local copies, waits for them, and re-layouts: 26.3 us -> 62.7 us
  blocking collectives: 77.1 us -> 43.1 us
  waiting for transfers between devices: 46 us -> 63.1 us
    unnamed x13 -> x66, local copies, waits for them, and re-layouts: 0.69 us -> 37.1 us
    ppermute x0 -> x15, starting transfers between devices: none -> 34.7 us  [the longest x7 34.5 us: set_the_patch(): odd.append(ppermute(odd[-1], axis_name=mesh_name, perm=ledger))]
    ppermute x0 -> x15, waiting for transfers between devices: none -> 32.7 us  [the longest x8 32.3 us: set_the_patch(): v_now.append(ppermute(v_now[-1], mesh_name, rows))]
    all_to_all x1 -> x0, blocking collectives: 30.8 us -> none  [copy_for_each(): return lax.all_to_all(copies, axis, split_axis=0, concat_axis=0, tiled=True)]
    all_gather x1 -> x0, waiting for transfers between devices: 15.8 us -> none  [shards(): lax.all_gather(owned_rows, 'row', axis=0, tiled=True)]
    all_to_all x0 -> x1, starting transfers between devices: none -> 14.8 us  [copy_for_each(): return lax.all_to_all(copies, axis, split_axis=0, concat_axis=0, tiled=True)]
    all_to_all x1, blocking collectives: 17.2 us -> 13.9 us  [shards(): lax.all_to_all(wanted, ('row', 'col'), split_axis=0, concat_axis=0, tiled...]
  transfers between devices with their start and end apart: 3 -> 18, of which waited for: 3 -> 10; matrix products, arithmetic and copies ran while one was open for 4% -> 16% of each run, Pallas kernels for 0% -> 0%
where the time goes in v1:
time: 287 us; the launch traced here: 286 us
  waiting for transfers between devices  63.1 us (22%)
  local copies, waits for them, and re-layouts  62.7 us (22%)
  starting transfers between devices  61.5 us (21%)
  blocking collectives  43.1 us (15%)
  matrix products  28.9 us (10%)
  between operations  13.7 us (5%)
  other arithmetic  12.9 us (4%)
    unnamed x66, local copies, waits for them, and re-layouts  37.1 us
    ppermute x7, starting transfers between devices, set_the_patch(): odd.append(ppermute(odd[-1], axis_name=mesh_name, perm=ledger))  34.5 us
    ppermute x8, waiting for transfers between devices, set_the_patch(): v_now.append(ppermute(v_now[-1], mesh_name, rows))  32.3 us
    all_to_all x1, blocking collectives, shards(): lax.all_to_all(owned_result[lax.all_to_all(wanted, ('row', 'col'), split_...  29.3 us
    dot_general x1, matrix products, add_block(): return jnp.dot(weighted, shard_rows, preferred_element_type=jnp.float32)  26.2 us
    reduce_scatter x1, waiting for transfers between devices, shards(): lax.psum_scatter(partial_sums, 'col', scatter_dimension=0, tiled=True)  17 us
    all_to_all x1, starting transfers between devices, copy_for_each(): return lax.all_to_all(copies, axis, split_axis=0, concat_axis=0, tiled=True)  14.8 us
    all_to_all x1, blocking collectives, shards(): lax.all_to_all(wanted, ('row', 'col'), split_axis=0, concat_axis=0, tiled...  13.9 us
  transfers between devices with their start and end apart: 18, of which 10 were waited for; matrix products, arithmetic and copies ran while one was open for 16% of the time, Pallas kernels for 0%

profile of v1, /device:TPU:1, one launch (start us, length us, event | category | flops | bytes accessed | tf_op | source)
XLA Modules:
  0.0 285.9 jit_solution(2334102191228378859)
XLA Ops:
  8.8 4.7 %gather_fusion = s32[768]{0:T(1024)S(1)} fusion(s32[32768]{0:T(1024)} %param.11, s32[1024]{0:T(1024)S(1)} %pad_clamp_fusion.2), kind=kCustom, calls=%fused_computation | custom fusion | bytes 9216 | tf_op jit(solution)/shard_map/gather | solution.py:53
  15.9 4.2 %gather_fusion.1 = s32[768]{0:T(1024)S(1)} fusion(s32[1,1024]{1,0:T(1,128)} %param.12, s32[768]{0:T(1024)S(1)} %fusion.18), kind=kCustom, calls=%fused_computation.1 | custom fusion | bytes 12288 | tf_op jit(solution)/shard_map/gather | solution.py:65
  20.2 3.3 %gather_fusion.2 = bf16[768,512]{1,0:T(8,128)(2,1)} fusion(bf16[1024,512]{1,0:T(8,128)(2,1)S(1)} %copy-done.2, s32[1024]{0:T(1024)S(1)} %pad_clamp_fusion.1), kind=kCustom, calls=%fused_computation.2 | custom fusion | bytes 1575936 | tf_op jit(solution)/shard_map/gather | solution.py:65
  26.2 12.0 %all-to-all-start = ((bf16[128,6,512]{2,1,0:T(8,128)(2,1)}), bf16[128,6,512]{2,1,0:T(8,128)(2,1)}, u32[]{:S(2)}, u32[]{:S(2)}) async-start(bf16[128,6,512]{2,1,0:T(8,128)(2,1)} %broadcast_select_fusion), calls=%async_computation | async-start | bytes 2097152 | tf_op jit(solution)/shard_map/all_to_all | solution.py:67
  38.2 4.6 %select_reduce_fusion = s32[256]{0:T(256)S(1)} fusion(s32[32768]{0:T(1024)S(1)} %copy-done.1, s32[256]{0:T(256)S(1)} %iota_add_fusion), kind=kLoop, calls=%fused_computation.6 | loop fusion | flops 25165568 | bytes 133120 | tf_op jit(solution)/shard_map/reduce_sum | solution.py:77
  43.7 13.4 %all-to-all-done = bf16[128,6,512]{2,1,0:T(8,128)(2,1)} async-done(((bf16[128,6,512]{2,1,0:T(8,128)(2,1)}), bf16[128,6,512]{2,1,0:T(8,128)(2,1)}, u32[]{:S(2)}, u32[]{:S(2)}) %all-to-all-start) | async-done | bytes 786464 | tf_op jit(solution)/shard_map/all_to_all | solution.py:67
  59.9 9.8 %collective-permute-done = bf16[256,512]{1,0:T(8,128)(2,1)S(1)} collective-permute-done((bf16[256,512]{1,0:T(8,128)(2,1)S(1)}, bf16[256,512]{1,0:T(8,128)(2,1)S(1)}, u32[]{:S(2)}, u32[]{:S(2)}) %collective-permute-start) | collective-permute-done | bytes 262176 | tf_op jit(solution)/shard_map/ppermute | solution.py:96
  69.7 4.8 %collective-permute-start.8 = (bf16[256,512]{1,0:T(8,128)(2,1)S(1)}, bf16[256,512]{1,0:T(8,128)(2,1)S(1)}, u32[]{:S(2)}, u32[]{:S(2)}) collective-permute-start(bf16[256,512]{1,0:T(8,128)(2,1)S(1)} %gather_fusion.3), channel_id=1, source_target_pairs={{0,120},{8,0},{16,8},{24,16},{32,24},{40,32},{48,40},{56,48},{64,5... | collective-permute-start | bytes 786440 | tf_op jit(solution)/shard_map/ppermute | solution.py:98
  74.5 4.2 %collective-permute-done.1 = bf16[256,512]{1,0:T(8,128)(2,1)S(1)} collective-permute-done((bf16[256,512]{1,0:T(8,128)(2,1)S(1)}, bf16[256,512]{1,0:T(8,128)(2,1)S(1)}, u32[]{:S(2)}, u32[]{:S(2)}) %collective-permute-start.1) | collective-permute-done | bytes 262176 | tf_op jit(solution)/shard_map/ppermute | solution.py:96
  78.7 4.8 %collective-permute-start.9 = (bf16[256,512]{1,0:T(8,128)(2,1)S(1)}, bf16[256,512]{1,0:T(8,128)(2,1)S(1)}, u32[]{:S(2)}, u32[]{:S(2)}) collective-permute-start(bf16[256,512]{1,0:T(8,128)(2,1)S(1)} %collective-permute-done.8), channel_id=1, source_target_pairs={{0,120},{8,0},{16,8},{24,16},{32,24},{40,32},{48,40},{56,48},{64,5... | collective-permute-start | bytes 786440 | tf_op jit(solution)/shard_map/ppermute | solution.py:98
  83.5 3.8 %collective-permute-done.2 = bf16[256,512]{1,0:T(8,128)(2,1)S(1)} collective-permute-done((bf16[256,512]{1,0:T(8,128)(2,1)S(1)}, bf16[256,512]{1,0:T(8,128)(2,1)S(1)}, u32[]{:S(2)}, u32[]{:S(2)}) %collective-permute-start.2) | collective-permute-done | bytes 262176 | tf_op jit(solution)/shard_map/ppermute | solution.py:96
  87.3 4.8 %collective-permute-start.10 = (bf16[256,512]{1,0:T(8,128)(2,1)S(1)}, bf16[256,512]{1,0:T(8,128)(2,1)S(1)}, u32[]{:S(2)}, u32[]{:S(2)}) collective-permute-start(bf16[256,512]{1,0:T(8,128)(2,1)S(1)} %collective-permute-done.9), channel_id=1, source_target_pairs={{0,120},{8,0},{16,8},{24,16},{32,24},{40,32},{48,40},{56,48},{64,5... | collective-permute-start | bytes 786440 | tf_op jit(solution)/shard_map/ppermute | solution.py:98
  92.0 3.8 %collective-permute-done.3 = bf16[256,512]{1,0:T(8,128)(2,1)S(1)} collective-permute-done((bf16[256,512]{1,0:T(8,128)(2,1)S(1)}, bf16[256,512]{1,0:T(8,128)(2,1)S(1)}, u32[]{:S(2)}, u32[]{:S(2)}) %collective-permute-start.3) | collective-permute-done | bytes 262176 | tf_op jit(solution)/shard_map/ppermute | solution.py:96
  95.8 4.8 %collective-permute-start.11 = (bf16[256,512]{1,0:T(8,128)(2,1)S(1)}, bf16[256,512]{1,0:T(8,128)(2,1)S(1)}, u32[]{:S(2)}, u32[]{:S(2)}) collective-permute-start(bf16[256,512]{1,0:T(8,128)(2,1)S(1)} %collective-permute-done.10), channel_id=1, source_target_pairs={{0,120},{8,0},{16,8},{24,16},{32,24},{40,32},{48,40},{56,48},{64,5... | collective-permute-start | bytes 786440 | tf_op jit(solution)/shard_map/ppermute | solution.py:98
  100.6 3.7 %collective-permute-done.4 = bf16[256,512]{1,0:T(8,128)(2,1)S(1)} collective-permute-done((bf16[256,512]{1,0:T(8,128)(2,1)S(1)}, bf16[256,512]{1,0:T(8,128)(2,1)S(1)}, u32[]{:S(2)}, u32[]{:S(2)}) %collective-permute-start.4) | collective-permute-done | bytes 262176 | tf_op jit(solution)/shard_map/ppermute | solution.py:96
  105.1 4.8 %collective-permute-start.12 = (bf16[256,512]{1,0:T(8,128)(2,1)S(1)}, bf16[256,512]{1,0:T(8,128)(2,1)}, u32[]{:S(2)}, u32[]{:S(2)}) collective-permute-start(bf16[256,512]{1,0:T(8,128)(2,1)S(1)} %collective-permute-done.11), channel_id=1, source_target_pairs={{0,120},{8,0},{16,8},{24,16},{32,24},{40,32},{48,40},{56,48},{64,5... | collective-permute-start | bytes 786440 | tf_op jit(solution)/shard_map/ppermute | solution.py:98
  109.9 3.0 %collective-permute-done.5 = bf16[256,512]{1,0:T(8,128)(2,1)S(1)} collective-permute-done((bf16[256,512]{1,0:T(8,128)(2,1)S(1)}, bf16[256,512]{1,0:T(8,128)(2,1)S(1)}, u32[]{:S(2)}, u32[]{:S(2)}) %collective-permute-start.5) | collective-permute-done | bytes 262176 | tf_op jit(solution)/shard_map/ppermute | solution.py:96
  113.2 5.3 %collective-permute-start.13 = (bf16[256,512]{1,0:T(8,128)(2,1)}, bf16[256,512]{1,0:T(8,128)(2,1)}, u32[]{:S(2)}, u32[]{:S(2)}) collective-permute-start(bf16[256,512]{1,0:T(8,128)(2,1)} %collective-permute-done.12), channel_id=1, source_target_pairs={{0,120},{8,0},{16,8},{24,16},{32,24},{40,32},{48,40},{56,48},{64,5... | collective-permute-start | bytes 786440 | tf_op jit(solution)/shard_map/ppermute | solution.py:98
  118.6 4.1 %collective-permute-done.6 = bf16[256,512]{1,0:T(8,128)(2,1)} collective-permute-done((bf16[256,512]{1,0:T(8,128)(2,1)S(1)}, bf16[256,512]{1,0:T(8,128)(2,1)}, u32[]{:S(2)}, u32[]{:S(2)}) %collective-permute-start.6) | collective-permute-done | bytes 262176 | tf_op jit(solution)/shard_map/ppermute | solution.py:96
  124.2 14.8 %all-to-all-start.1 = ((bf16[8,256,512]{2,1,0:T(8,128)(2,1)}), bf16[8,256,512]{2,1,0:T(8,128)(2,1)}, u32[]{:S(2)}, u32[]{:S(2)}) async-start(bf16[8,256,512]{2,1,0:T(8,128)(2,1)} %broadcast_in_dim.79), calls=%async_computation.1 | async-start | bytes 4194304 | tf_op jit(solution)/shard_map/all_to_all | solution.py:15
  139.1 5.1 %collective-permute-start.14 = (bf16[256,512]{1,0:T(8,128)(2,1)}, bf16[256,512]{1,0:T(8,128)(2,1)S(1)}, u32[]{:S(2)}, u32[]{:S(2)}) collective-permute-start(bf16[256,512]{1,0:T(8,128)(2,1)} %collective-permute-done.13), channel_id=1, source_target_pairs={{0,120},{8,0},{16,8},{24,16},{32,24},{40,32},{48,40},{56,48},{64,5... | collective-permute-start | bytes 786440 | tf_op jit(solution)/shard_map/ppermute | solution.py:98
  150.9 1.7 constant_dynamic-update-slice_fusion.27
  152.6 1.7 constant_dynamic-update-slice_fusion.26
  157.9 1.7 constant_dynamic-update-slice_fusion.20
  159.6 1.7 constant_dynamic-update-slice_fusion.19
  180.7 26.2 %fusion = f32[2048,512]{1,0:T(8,128)} fusion(bf16[2048,4096]{1,0:T(8,128)(2,1)} %param.8, bf16[8192,512]{1,0:T(8,128)(2,1)} %constant_dynamic-update-slice_fusion, s32[]{:T(128)S(6)} %select_n.119, bf16[2048,512]{1,0:T(8,128)(2,1)} %bitcast.3), kind=kOutput, calls=%fused_computation.7 | convolution fusion | flops 17221812224 | bytes 31458304 | tf_op jit(solution)/shard_map/dot_general | solution.py:36
  208.2 13.9 %all_to_all.27 = s32[128,1,8]{2,1,0:T(1,128)S(1)} all-to-all(s32[128,1,8]{2,1,0:T(1,128)S(1)} %bitcast.17), channel_id=1, replica_groups=mesh['row'=16,'col'=8] {'row','col'}, dimensions={0} | all-to-all | bytes 8192 | tf_op jit(solution)/shard_map/all_to_all | solution.py:110
  222.2 17.0 %reduce-scatter.2.cloned.1.call-done = f32[256,512]{1,0:T(8,128)} async-done(((f32[2048,512]{1,0:T(8,128)}), f32[256,512]{1,0:T(8,128)}) %reduce-scatter.2.cloned.1.call-update) | async-done | bytes 524304 | tf_op jit(solution)/shard_map/reduce_scatter | solution.py:104
  240.3 4.0 %gather_fusion.4 = bf16[1024,512]{1,0:T(8,128)(2,1)S(1)} fusion(bf16[256,512]{1,0:T(8,128)(2,1)S(1)} %convert_element_type.31, s32[1024]{0:T(1024)S(1)} %broadcast_clamp_fusion), kind=kCustom, calls=%fused_computation.4 | custom fusion | bytes 2101248 | tf_op jit(solution)/shard_map/gather | solution.py:109
  244.2 29.3 %all_to_all.28 = bf16[128,8,512]{2,1,0:T(8,128)(2,1)S(1)} all-to-all(bf16[128,8,512]{2,1,0:T(8,128)(2,1)S(1)} %bitcast.16), channel_id=1, replica_groups=mesh['row'=16,'col'=8] {'row','col'}, dimensions={0} | all-to-all | bytes 2097152 | tf_op jit(solution)/shard_map/all_to_all | solution.py:108
  273.5 2.7 negate_bitcast_fusion
  276.2 2.9 %copy.17 = f32[1024,512]{1,0:T(8,128)} copy(f32[1024,512]{0,1:T(8,128)} %negate_bitcast_fusion) | data formatting | bytes 4194304 | tf_op jit(solution)/shard_map/neg | solution.py:118
  (115 shorter events, 45.8 us)
Async XLA Ops:
  6.5 267.0 %copy-start = (bf16[1024,1024]{1,0:T(8,128)(2,1)S(1)}, bf16[1024,1024]{1,0:T(8,128)(2,1)}, u32[]{:S(2)}) copy-start(bf16[1024,1024]{1,0:T(8,128)(2,1)} %param.9) | copy-start | bytes 6291460
  6.5 13.7 %copy-start.2 = (bf16[1024,512]{1,0:T(8,128)(2,1)S(1)}, bf16[1024,512]{1,0:T(8,128)(2,1)}, u32[]{:S(2)}) copy-start(bf16[1024,512]{1,0:T(8,128)(2,1)} %param.7) | copy-start | bytes 3145732
  15.9 22.3 %copy-start.1 = (s32[32768]{0:T(1024)S(1)}, s32[32768]{0:T(1024)}, u32[]{:S(2)}) copy-start(s32[32768]{0:T(1024)} %param.11) | copy-start | bytes 393220
  15.9 26.9 %copy-start.16 = (s32[128]{0:T(128)S(1)}, s32[128]{0:T(128)}, u32[]{:S(2)}) copy-start(s32[128]{0:T(128)} %param.10) | copy-start | bytes 1540
  26.2 30.9 %all-to-all-start = ((bf16[128,6,512]{2,1,0:T(8,128)(2,1)}), bf16[128,6,512]{2,1,0:T(8,128)(2,1)}, u32[]{:S(2)}, u32[]{:S(2)}) async-start(bf16[128,6,512]{2,1,0:T(8,128)(2,1)} %broadcast_select_fusion), calls=%async_computation | async-start | bytes 2097152 | tf_op jit(solution)/shard_map/all_to_all | solution.py:67
  59.6 10.0 %collective-permute-start = (bf16[256,512]{1,0:T(8,128)(2,1)S(1)}, bf16[256,512]{1,0:T(8,128)(2,1)S(1)}, u32[]{:S(2)}, u32[]{:S(2)}) collective-permute-start(bf16[256,512]{1,0:T(8,128)(2,1)S(1)} %gather_fusion.3), channel_id=1, source_target_pairs={{0,8},{8,16},{16,24},{24,32},{32,40},{40,48},{48,56},{56,64},{64,7... | collective-permute-start | bytes 786440 | tf_op jit(solution)/shard_map/ppermute | solution.py:96
  69.7 9.0 %collective-permute-start.1 = (bf16[256,512]{1,0:T(8,128)(2,1)S(1)}, bf16[256,512]{1,0:T(8,128)(2,1)S(1)}, u32[]{:S(2)}, u32[]{:S(2)}) collective-permute-start(bf16[256,512]{1,0:T(8,128)(2,1)S(1)} %collective-permute-done), channel_id=1, source_target_pairs={{0,8},{8,16},{16,24},{24,32},{32,40},{40,48},{48,56},{56,64},{64,7... | collective-permute-start | bytes 786440 | tf_op jit(solution)/shard_map/ppermute | solution.py:96
  69.7 9.0 %collective-permute-start.8 = (bf16[256,512]{1,0:T(8,128)(2,1)S(1)}, bf16[256,512]{1,0:T(8,128)(2,1)S(1)}, u32[]{:S(2)}, u32[]{:S(2)}) collective-permute-start(bf16[256,512]{1,0:T(8,128)(2,1)S(1)} %gather_fusion.3), channel_id=1, source_target_pairs={{0,120},{8,0},{16,8},{24,16},{32,24},{40,32},{48,40},{56,48},{64,5... | collective-permute-start | bytes 786440 | tf_op jit(solution)/shard_map/ppermute | solution.py:98
  78.7 8.5 %collective-permute-start.2 = (bf16[256,512]{1,0:T(8,128)(2,1)S(1)}, bf16[256,512]{1,0:T(8,128)(2,1)S(1)}, u32[]{:S(2)}, u32[]{:S(2)}) collective-permute-start(bf16[256,512]{1,0:T(8,128)(2,1)S(1)} %collective-permute-done.1), channel_id=1, source_target_pairs={{0,8},{8,16},{16,24},{24,32},{32,40},{40,48},{48,56},{56,64},{64,7... | collective-permute-start | bytes 786440 | tf_op jit(solution)/shard_map/ppermute | solution.py:96
  78.7 8.5 %collective-permute-start.9 = (bf16[256,512]{1,0:T(8,128)(2,1)S(1)}, bf16[256,512]{1,0:T(8,128)(2,1)S(1)}, u32[]{:S(2)}, u32[]{:S(2)}) collective-permute-start(bf16[256,512]{1,0:T(8,128)(2,1)S(1)} %collective-permute-done.8), channel_id=1, source_target_pairs={{0,120},{8,0},{16,8},{24,16},{32,24},{40,32},{48,40},{56,48},{64,5... | collective-permute-start | bytes 786440 | tf_op jit(solution)/shard_map/ppermute | solution.py:98
  87.2 8.5 %collective-permute-start.3 = (bf16[256,512]{1,0:T(8,128)(2,1)S(1)}, bf16[256,512]{1,0:T(8,128)(2,1)S(1)}, u32[]{:S(2)}, u32[]{:S(2)}) collective-permute-start(bf16[256,512]{1,0:T(8,128)(2,1)S(1)} %collective-permute-done.2), channel_id=1, source_target_pairs={{0,8},{8,16},{16,24},{24,32},{32,40},{40,48},{48,56},{56,64},{64,7... | collective-permute-start | bytes 786440 | tf_op jit(solution)/shard_map/ppermute | solution.py:96
  87.3 8.5 %collective-permute-start.10 = (bf16[256,512]{1,0:T(8,128)(2,1)S(1)}, bf16[256,512]{1,0:T(8,128)(2,1)S(1)}, u32[]{:S(2)}, u32[]{:S(2)}) collective-permute-start(bf16[256,512]{1,0:T(8,128)(2,1)S(1)} %collective-permute-done.9), channel_id=1, source_target_pairs={{0,120},{8,0},{16,8},{24,16},{32,24},{40,32},{48,40},{56,48},{64,5... | collective-permute-start | bytes 786440 | tf_op jit(solution)/shard_map/ppermute | solution.py:98
  95.8 17.4 %copy-start.9 = (bf16[256,512]{1,0:T(8,128)(2,1)}, bf16[256,512]{1,0:T(8,128)(2,1)S(1)}, u32[]{:S(2)}) copy-start(bf16[256,512]{1,0:T(8,128)(2,1)S(1)} %collective-permute-done.3) | copy-start | bytes 786436
  95.8 8.5 %collective-permute-start.4 = (bf16[256,512]{1,0:T(8,128)(2,1)S(1)}, bf16[256,512]{1,0:T(8,128)(2,1)S(1)}, u32[]{:S(2)}, u32[]{:S(2)}) collective-permute-start(bf16[256,512]{1,0:T(8,128)(2,1)S(1)} %collective-permute-done.3), channel_id=1, source_target_pairs={{0,8},{8,16},{16,24},{24,32},{32,40},{40,48},{48,56},{56,64},{64,7... | collective-permute-start | bytes 786440 | tf_op jit(solution)/shard_map/ppermute | solution.py:96
  95.8 8.5 %collective-permute-start.11 = (bf16[256,512]{1,0:T(8,128)(2,1)S(1)}, bf16[256,512]{1,0:T(8,128)(2,1)S(1)}, u32[]{:S(2)}, u32[]{:S(2)}) collective-permute-start(bf16[256,512]{1,0:T(8,128)(2,1)S(1)} %collective-permute-done.10), channel_id=1, source_target_pairs={{0,120},{8,0},{16,8},{24,16},{32,24},{40,32},{48,40},{56,48},{64,5... | collective-permute-start | bytes 786440 | tf_op jit(solution)/shard_map/ppermute | solution.py:98
  104.3 14.2 %copy-start.11 = (bf16[256,512]{1,0:T(8,128)(2,1)}, bf16[256,512]{1,0:T(8,128)(2,1)S(1)}, u32[]{:S(2)}) copy-start(bf16[256,512]{1,0:T(8,128)(2,1)S(1)} %collective-permute-done.4) | copy-start | bytes 786436
  104.3 8.6 %collective-permute-start.5 = (bf16[256,512]{1,0:T(8,128)(2,1)S(1)}, bf16[256,512]{1,0:T(8,128)(2,1)S(1)}, u32[]{:S(2)}, u32[]{:S(2)}) collective-permute-start(bf16[256,512]{1,0:T(8,128)(2,1)S(1)} %collective-permute-done.4), channel_id=1, source_target_pairs={{0,8},{8,16},{16,24},{24,32},{32,40},{40,48},{48,56},{56,64},{64,7... | collective-permute-start | bytes 786440 | tf_op jit(solution)/shard_map/ppermute | solution.py:96
  105.1 8.1 %collective-permute-start.12 = (bf16[256,512]{1,0:T(8,128)(2,1)S(1)}, bf16[256,512]{1,0:T(8,128)(2,1)}, u32[]{:S(2)}, u32[]{:S(2)}) collective-permute-start(bf16[256,512]{1,0:T(8,128)(2,1)S(1)} %collective-permute-done.11), channel_id=1, source_target_pairs={{0,120},{8,0},{16,8},{24,16},{32,24},{40,32},{48,40},{56,48},{64,5... | collective-permute-start | bytes 786440 | tf_op jit(solution)/shard_map/ppermute | solution.py:98
  112.9 9.8 %copy-start.13 = (bf16[256,512]{1,0:T(8,128)(2,1)}, bf16[256,512]{1,0:T(8,128)(2,1)S(1)}, u32[]{:S(2)}) copy-start(bf16[256,512]{1,0:T(8,128)(2,1)S(1)} %collective-permute-done.5) | copy-start | bytes 786436
  112.9 9.8 %collective-permute-start.6 = (bf16[256,512]{1,0:T(8,128)(2,1)S(1)}, bf16[256,512]{1,0:T(8,128)(2,1)}, u32[]{:S(2)}, u32[]{:S(2)}) collective-permute-start(bf16[256,512]{1,0:T(8,128)(2,1)S(1)} %collective-permute-done.5), channel_id=1, source_target_pairs={{0,8},{8,16},{16,24},{24,32},{32,40},{40,48},{48,56},{56,64},{64,7... | collective-permute-start | bytes 786440 | tf_op jit(solution)/shard_map/ppermute | solution.py:96
  113.2 25.8 %collective-permute-start.13 = (bf16[256,512]{1,0:T(8,128)(2,1)}, bf16[256,512]{1,0:T(8,128)(2,1)}, u32[]{:S(2)}, u32[]{:S(2)}) collective-permute-start(bf16[256,512]{1,0:T(8,128)(2,1)} %collective-permute-done.12), channel_id=1, source_target_pairs={{0,120},{8,0},{16,8},{24,16},{32,24},{40,32},{48,40},{56,48},{64,5... | collective-permute-start | bytes 786440 | tf_op jit(solution)/shard_map/ppermute | solution.py:98
  122.7 21.5 %collective-permute-start.7 = (bf16[256,512]{1,0:T(8,128)(2,1)}, bf16[256,512]{1,0:T(8,128)(2,1)}, u32[]{:S(2)}, u32[]{:S(2)}) collective-permute-start(bf16[256,512]{1,0:T(8,128)(2,1)} %collective-permute-done.6), channel_id=1, source_target_pairs={{0,8},{8,16},{16,24},{24,32},{32,40},{40,48},{48,56},{56,64},{64,7... | collective-permute-start | bytes 786440 | tf_op jit(solution)/shard_map/ppermute | solution.py:96
  124.2 56.5 %all-to-all-start.1 = ((bf16[8,256,512]{2,1,0:T(8,128)(2,1)}), bf16[8,256,512]{2,1,0:T(8,128)(2,1)}, u32[]{:S(2)}, u32[]{:S(2)}) async-start(bf16[8,256,512]{2,1,0:T(8,128)(2,1)} %broadcast_in_dim.79), calls=%async_computation.1 | async-start | bytes 4194304 | tf_op jit(solution)/shard_map/all_to_all | solution.py:15
  139.0 100.2 %reduce-scatter.2.cloned.1.call-start = ((), (), s32[]{:S(2)}) async-start(), calls=%async_computation.5 | async-start | bytes 4718592 | tf_op jit(solution)/shard_map/reduce_scatter | solution.py:104
  139.0 29.6 %copy-start.14 = (bf16[256,512]{1,0:T(8,128)(2,1)S(1)}, bf16[256,512]{1,0:T(8,128)(2,1)}, u32[]{:S(2)}) copy-start(bf16[256,512]{1,0:T(8,128)(2,1)} %copy-done.13) | copy-start | bytes 786436
  139.0 30.4 %copy-start.12 = (bf16[256,512]{1,0:T(8,128)(2,1)S(1)}, bf16[256,512]{1,0:T(8,128)(2,1)}, u32[]{:S(2)}) copy-start(bf16[256,512]{1,0:T(8,128)(2,1)} %copy-done.11) | copy-start | bytes 786436
  139.0 31.1 %copy-start.10 = (bf16[256,512]{1,0:T(8,128)(2,1)S(1)}, bf16[256,512]{1,0:T(8,128)(2,1)}, u32[]{:S(2)}) copy-start(bf16[256,512]{1,0:T(8,128)(2,1)} %copy-done.9) | copy-start | bytes 786436
  139.0 31.8 %copy-start.4 = (bf16[256,512]{1,0:T(8,128)(2,1)S(1)}, bf16[256,512]{1,0:T(8,128)(2,1)}, u32[]{:S(2)}) copy-start(bf16[256,512]{1,0:T(8,128)(2,1)} %copy-done.3) | copy-start | bytes 786436
  139.1 36.2 %copy-start.6 = (bf16[256,512]{1,0:T(8,128)(2,1)S(1)}, bf16[256,512]{1,0:T(8,128)(2,1)}, u32[]{:S(2)}) copy-start(bf16[256,512]{1,0:T(8,128)(2,1)} %copy-done.5) | copy-start | bytes 786436
  139.1 36.9 %copy-start.8 = (bf16[256,512]{1,0:T(8,128)(2,1)S(1)}, bf16[256,512]{1,0:T(8,128)(2,1)}, u32[]{:S(2)}) copy-start(bf16[256,512]{1,0:T(8,128)(2,1)} %copy-done.7) | copy-start | bytes 786436
  139.1 25.5 %collective-permute-start.14 = (bf16[256,512]{1,0:T(8,128)(2,1)}, bf16[256,512]{1,0:T(8,128)(2,1)S(1)}, u32[]{:S(2)}, u32[]{:S(2)}) collective-permute-start(bf16[256,512]{1,0:T(8,128)(2,1)} %collective-permute-done.13), channel_id=1, source_target_pairs={{0,120},{8,0},{16,8},{24,16},{32,24},{40,32},{48,40},{56,48},{64,5... | collective-permute-start | bytes 786440 | tf_op jit(solution)/shard_map/ppermute | solution.py:98
  180.7 26.8 %copy-start.15 = (s32[1,1024]{1,0:T(1,128)S(1)}, s32[1,1024]{1,0:T(1,128)}, u32[]{:S(2)}) copy-start(s32[1,1024]{1,0:T(1,128)} %param.13) | copy-start | bytes 12292
  (3 other events, 14.2 us)
Sparse Core Ops, SparseCore 0:
  207.1 32.0 reduce-scatter.1
